TPU v7x, 256 devices: a whole 4x4x8 slice. The times are simulated.
256 devices in a mesh: row: 32 (over y_hi, z, core), col: 8 (over y_lo, x).
Axes of the slice: x: 4, y: 4 (y_hi: 2, y_lo: 2; y = y_hi * 2 + y_lo), z: 8, core: 2. Of those that a mesh axis runs over, the one named last changes fastest.
Arguments:
- hamiltonian: float32 [24576, 24576], P('row', 'col'), may hold values from -2 to 2, as said below
- vectors: float32 [24576, 512], P(('row', 'col')), may hold values from -6 to 6
Outputs:
- filtered: float32 [24576, 512], P(('row', 'col'))
Inputs may be any that keep to these rules, and one draw needn't show every extreme that they name: `hamiltonian`: exactly symmetric, with a diagonal part and a dense part of comparable weight.
All inputs are finite; a program needn't handle non-finite values.
Results may differ from a plain program's by a relative error of at most 0.0001.
Values sent between devices are 32-bit elements; how exact they have to be, the bound alone decides.
A program may use at most 64 MiB of HBM per device.

v0:
```python
import jax
import jax.numpy as jnp
from jax import lax
from jax.sharding import PartitionSpec as P

DEGREE = 2


center = 0.6
half_width = 1.8


def transposed_product(left, right):
    return lax.dot_general(
        left,
        right,
        (((0,), (0,)), ((), ())),
        precision=lax.Precision.HIGHEST,
        preferred_element_type=jnp.float32,
    )


def plain_product(left, right):
    return jnp.dot(left, right, precision=lax.Precision.HIGHEST, preferred_element_type=jnp.float32)


def on_device(hamiltonian, vectors):
    row_index = lax.axis_index("row")
    col_index = lax.axis_index("col")
    rows_block, cols_block = hamiltonian.shape
    global_rows = row_index * rows_block + lax.iota(jnp.int32, rows_block)
    global_cols = col_index * cols_block + lax.iota(jnp.int32, cols_block)
    on_diagonal = global_rows[:, None] == global_cols[None, :]
    shifted = hamiltonian - jnp.where(on_diagonal, jnp.float32(center), jnp.float32(0.0))
    older = vectors
    recent = vectors
    for degree in range(1, DEGREE + 1):
        if degree % 2 == 1:
            row_block = lax.all_gather(recent, "col", axis=0, tiled=True)
            total = lax.psum_scatter(
                transposed_product(shifted, row_block), "row", scatter_dimension=0, tiled=True
            )
        else:
            partial_sum = plain_product(shifted, lax.all_gather(recent, "row", axis=0, tiled=True))
            total = lax.psum_scatter(partial_sum, "col", scatter_dimension=0, tiled=True)
        if degree == 1:
            fresh = total * (1.0 / half_width)
        else:
            fresh = 2.0 / half_width * total - older
        older = recent
        recent = fresh
    return recent


def solution(mesh):
    return jax.shard_map(
        on_device,
        mesh=mesh,
        in_specs=(P("row", "col"), P(("row", "col"), None)),
        out_specs=P(("row", "col"), None),
        check_vma=False,
    )
```

profile of v0, /device:TPU:1, one launch (start us, length us, event | category | flops | bytes accessed | tf_op | source)
XLA Modules:
  0.0 370.0 jit_solution(8472864970805177196)
XLA Ops:
  6.5 0.0 all-gather.3.cloned.1.call-start
  6.5 0.7 all-gather.3.cloned.1.call-update
  7.3 0.0 reduce-scatter.3.cloned.1.call-start
  7.3 42.1 %all-gather.3.cloned.1.call-done = f32[768,512]{1,0:T(8,128)} async-done(((f32[96,512]{1,0:T(8,128)}), f32[768,512]{1,0:T(8,128)}) %all-gather.3.cloned.1.call-update) | async-done | bytes 1572880 | tf_op jit(solution)/shard_map/all_gather | solution.py:39
  49.5 19.8 %fusion.1 = f32[3072,512]{1,0:T(8,128)} fusion(f32[768,512]{1,0:T(8,128)} %all-gather.3.cloned.1.call-done, f32[768,3072]{1,0:T(8,128)} %param.2, s32[3072]{0:T(1024)S(1)} %iota_add_fusion, s32[768]{0:T(1024)S(1)} %iota_add_fusion.1), kind=kOutput, calls=%fused_computation.2 | convolution fusion | flops 14502592512 | bytes 17316864 | tf_op jit(solution)/shard_map/dot_general | solution.py:14
  69.3 0.0 reduce-scatter.3.cloned.1.call-update
  69.3 0.0 all-gather.5.cloned.1.call-start
  69.4 138.8 %reduce-scatter.3.cloned.1.call-done = f32[96,512]{1,0:T(8,128)} async-done(((f32[3072,512]{1,0:T(8,128)}), f32[96,512]{1,0:T(8,128)}) %reduce-scatter.3.cloned.1.call-update) | async-done | bytes 196624 | tf_op jit(solution)/shard_map/reduce_scatter | solution.py:40
  208.1 1.6 broadcast_multiply_fusion
  209.8 0.0 all-gather.5.cloned.1.call-update
  209.8 0.0 copy-start
  209.8 0.2 reduce-scatter.5.cloned.1.call-start
  210.0 97.0 %all-gather.5.cloned.1.call-done = f32[3072,512]{1,0:T(8,128)} async-done(((f32[96,512]{1,0:T(8,128)}), f32[3072,512]{1,0:T(8,128)}) %all-gather.5.cloned.1.call-update) | async-done | bytes 6291472 | tf_op jit(solution)/shard_map/all_gather | solution.py:44
  307.0 20.2 %fusion = f32[768,512]{1,0:T(8,128)} fusion(f32[3072,512]{1,0:T(8,128)} %all-gather.5.cloned.1.call-done, f32[768,3072]{1,0:T(8,128)} %param.2, s32[3072]{0:T(1024)S(1)} %iota_add_fusion, s32[768]{0:T(1024)S(1)} %iota_add_fusion.1), kind=kOutput, calls=%fused_computation.1 | convolution fusion | flops 14502592512 | bytes 17316864 | tf_op jit(solution)/shard_map/dot_general | solution.py:24
  327.2 0.0 reduce-scatter.5.cloned.1.call-update
  327.2 34.6 %reduce-scatter.5.cloned.1.call-done = f32[96,512]{1,0:T(8,128)} async-done(((f32[768,512]{1,0:T(8,128)}), f32[96,512]{1,0:T(8,128)}) %reduce-scatter.5.cloned.1.call-update) | async-done | bytes 196624 | tf_op jit(solution)/shard_map/reduce_scatter | solution.py:45
  361.9 0.0 copy-done
  361.9 1.6 multiply_subtract_fusion
  (2 shorter events, 0.0 us)
Async XLA Ops:
  6.5 42.9 %all-gather.3.cloned.1.call-start = ((), (), s32[]{:S(2)}) async-start(), calls=%async_computation.2 | async-start | bytes 1769472 | tf_op jit(solution)/shard_map/all_gather | solution.py:39
  7.3 200.9 %reduce-scatter.3.cloned.1.call-start = ((), (), s32[]{:S(2)}) async-start(), calls=%async_computation.3 | async-start | bytes 6488064 | tf_op jit(solution)/shard_map/reduce_scatter | solution.py:40
  69.3 237.7 %all-gather.5.cloned.1.call-start = ((), (), s32[]{:S(2)}) async-start(), calls=%async_computation.4 | async-start | bytes 6488064 | tf_op jit(solution)/shard_map/all_gather | solution.py:44
  209.8 152.1 %copy-start = (f32[96,512]{1,0:T(8,128)S(1)}, f32[96,512]{1,0:T(8,128)}, u32[]{:S(2)}) copy-start(f32[96,512]{1,0:T(8,128)} %param.3) | copy-start | bytes 589828
  209.8 152.1 %reduce-scatter.5.cloned.1.call-start = ((), (), s32[]{:S(2)}) async-start(), calls=%async_computation.5 | async-start | bytes 1769472 | tf_op jit(solution)/shard_map/reduce_scatter | solution.py:45
Sparse Core Ops, SparseCore 0:
  9.1 40.3 all-gather.2
  69.4 138.6 reduce-scatter.2
  210.9 96.0 all-gather.4
  327.3 34.4 reduce-scatter.4
where the time goes:
time: 374 us; the launch traced here: 370 us
  waiting for transfers between devices  313 us (84%)
  matrix products  40 us (11%)
  between operations  13.2 us (4%)
    reduce_scatter x1, waiting for transfers between devices, on_device(): lax.psum_scatter(transposed_product(shifted, row_block), 'row', scatter_d...  139 us
    all_gather x1, waiting for transfers between devices, on_device(): lax.all_gather(recent, 'row', axis=0, tiled=True)  97 us
    all_gather x1, waiting for transfers between devices, on_device(): row_block = lax.all_gather(recent, 'col', axis=0, tiled=True)  42.1 us
    reduce_scatter x1, waiting for transfers between devices, on_device(): lax.psum_scatter(partial_sum, 'col', scatter_dimension=0, tiled=True)  34.6 us
    dot_general x1, matrix products, plain_product(): jnp.dot(left, right, precision=lax.Precision.HIGHEST, preferred_element_t...  20.2 us
    dot_general x1, matrix products, transposed_product(): lax.dot_general(left, right, (((0,), (0,)), ((), ())), precision=lax.Prec...  19.8 us
  transfers between devices with their start and end apart: 4, of which 4 were waited for; matrix products, arithmetic and copies ran while one was open for 0% of the time, Pallas kernels for 0%

commit v1 on v0

v1 whole, which is shorter than its diff:
```python
import functools

import jax
import jax.numpy as jnp
from jax import lax
from jax.experimental import pallas as pl
from jax.experimental.pallas import tpu as pltpu
from jax.sharding import PartitionSpec as P

MESH = pl.DeviceIdType.MESH
F32 = jnp.float32
BF16 = jnp.bfloat16

CENTER = 0.6
HALF_WIDTH = 1.8

CHUNKS = 4
WIDE = 128
ROWS, COLS = 768, 3072
HALF = COLS // 2
OWN = 96
PIECES = 8
TILE = 512

READY = (0, 3, 5, 8, 13, 17, 21, 25, 29, 33, 36.5, 40, 43.5, 45, 47, 51, 54, 57)
APART = 8.0


def split(value):
    high = value.astype(BF16)
    return high, (value - high.astype(F32)).astype(BF16)


def kernel(h_ref, v_ref, o_ref, h_in, h_hi, h_lo, y0, cat0, p1, cr, zr, yb, yr, y1, cat1, p2, xr, xb, lr,
           h_sem, send_sem, recv_sem):
    row, col = lax.axis_index("row"), lax.axis_index("col")
    core, z, y_hi = lax.rem(row, 2), lax.rem(row // 2, 8), row // 16
    x, y_lo = lax.rem(col, 4), col // 4

    def at_z(k):
        return lax.rem(z + k, 8)

    def at_x(k):
        return lax.rem(x + k, 4)

    z_up = (y_hi * 16 + at_z(1) * 2 + core, col)
    z_down = (y_hi * 16 + at_z(7) * 2 + core, col)
    sibling = (row + 1 - 2 * core, col)
    y_far = (lax.rem(row + 16, 32), col)
    x_up = (row, y_lo * 4 + at_x(1))
    x_down = (row, y_lo * 4 + at_x(3))
    y_near = (row, lax.rem(col + 4, 8))
    partners = (z_up, z_down, sibling, y_far, x_up, x_down, y_near)

    loads = [
        pltpu.make_async_copy(h_ref.at[pl.ds(OWN * i, OWN), :], h_in.at[i], h_sem.at[i]) for i in range(PIECES)
    ]
    for load in loads:
        load.start()

    barrier = pltpu.get_barrier_semaphore()
    for partner in partners:
        pl.semaphore_signal(barrier, inc=1, device_id=partner, device_id_type=MESH)
    pl.semaphore_wait(barrier, len(partners))

    started = {}

    def send(key, src, dst, device):
        n = len(started)
        copy = pltpu.make_async_remote_copy(
            src_ref=src, dst_ref=dst, send_sem=send_sem.at[n], recv_sem=recv_sem.at[n],
            device_id=device, device_id_type=MESH,
        )
        copy.start()
        started[key] = copy

    def arrived(*key):
        started[key].wait_recv()

    def slot(other, k):
        return (y_lo + other - 2 * other * y_lo) * 4 + at_x(k)

    def lanes(q):
        return pl.ds(WIDE * q, WIDE)

    def gather_0(q):
        y0[q, col] = v_ref[:, lanes(q)]
        own = v_ref.at[:, lanes(q)]
        for n, device in enumerate((y_near, x_up, x_down)):
            send((q, "a", n), own, y0.at[q, col], device)

    def gather_1(q):
        arrived(q, "a", 0)
        other = y0.at[q, slot(1, 0)]
        send((q, "a", 3), other, other, x_up)
        send((q, "a", 4), other, other, x_down)

    def gather_2(q):
        arrived(q, "a", 1)
        piece = y0.at[q, slot(0, 3)]
        send((q, "a", 5), piece, piece, x_up)
        arrived(q, "a", 4)
        piece = y0.at[q, slot(1, 1)]
        send((q, "a", 6), piece, piece, x_down)

    def product_1(q):
        for n in (2, 3, 5, 6):
            arrived(q, "a", n)
        high, low = split(y0[q].reshape(ROWS, WIDE).T)
        cat0[0:WIDE, :] = high
        cat0[WIDE:, :] = low

        def half_of(half):
            def step(j, carry):
                at = pl.multiple_of(half * HALF + j * TILE, 128)
                both = jnp.dot(cat0[...], h_hi[:, pl.ds(at, TILE)], preferred_element_type=F32)
                rest = jnp.dot(cat0[0:WIDE, :], h_lo[:, pl.ds(at, TILE)], preferred_element_type=F32)
                value = both[:WIDE] + (both[WIDE:] + rest)
                p1[q, half, :, :, pl.ds(pl.multiple_of(j * TILE, 128), TILE)] = value.reshape(8, 16, TILE)
                return carry

            lax.fori_loop(0, HALF // TILE, step, 0)

        half_of(1 - core)
        send((q, "c"), p1.at[q, 1 - core], cr.at[q], sibling)
        half_of(core)

    def scatter_0(q):
        arrived(q, "c")
        far = at_z(4)
        p1[q, core, far] = p1[q, core, far] + cr[q, far]
        send((q, "r", 0, 1), p1.at[q, core, far, pl.ds(0, 8)], zr.at[q, 0, 0, pl.ds(0, 8)], z_up)
        send((q, "r", 1, 1), p1.at[q, core, far, pl.ds(8, 8)], zr.at[q, 1, 0, pl.ds(8, 8)], z_down)

    def scatter(step, q):
        for way, device in ((0, z_up), (1, z_down)):
            to = at_z(5 - step) if way == 0 else at_z(3 + step)
            arrived(q, "r", way, step - 1)
            if step == 2:
                first, second = pl.ds(8 * way, 8), pl.ds(8 - 8 * way, 8)
                p1[q, core, to, first] = p1[q, core, to, first] + cr[q, to, first] + zr[q, way, 0, first]
                p1[q, core, to, second] = p1[q, core, to, second] + cr[q, to, second]
            else:
                p1[q, core, to] = p1[q, core, to] + cr[q, to] + zr[q, way, step - 2]
            send((q, "r", way, step), p1.at[q, core, to], zr.at[q, way, step - 1], device)

    def scatter_y(q):
        arrived(q, "r", 0, 4)
        arrived(q, "r", 1, 4)
        yb[q] = p1[q, core, z] + cr[q, z] + (zr[q, 0, 3] + zr[q, 1, 3])
        send((q, "y"), yb.at[q], yr.at[q], y_far)

    def pass_on(q, k, part=slice(None)):
        piece = y1.at[q, core, at_z(k)] if part == slice(None) else y1.at[q, core, at_z(k), pl.ds(part, 8)]
        return piece

    def spread_0(q):
        arrived(q, "y")
        y1[q, core, z] = (yb[q] + yr[q]) * (1.0 / HALF_WIDTH)
        piece = pass_on(q, 0)
        send((q, "g", 0, 1), piece, piece, z_up)
        send((q, "g", 1, 1), piece, piece, z_down)
        send((q, "d", 0), piece, piece, sibling)

    def spread(step, q):
        for way, device in ((0, z_up), (1, z_down)):
            arrived(q, "g", way, step - 1)
            k = 9 - step if way == 0 else step - 1
            piece = pass_on(q, k) if step < 4 else pass_on(q, k, 8 * way)
            send((q, "g", way, step), piece, piece, device)
            piece = pass_on(q, k)
            send((q, "d", k), piece, piece, sibling)

    def spread_last(q):
        arrived(q, "g", 0, 4)
        arrived(q, "g", 1, 4)
        piece = pass_on(q, 4)
        send((q, "d", 4), piece, piece, sibling)

    def product_2(q):
        for k in range(8):
            arrived(q, "d", k)
        for half in range(2):
            high, low = split(y1[q, half].reshape(WIDE, HALF))
            cat1[0:WIDE, pl.ds(half * HALF, HALF)] = high
            cat1[WIDE:, pl.ds(half * HALF, HALF)] = low

        def step(i, carry):
            at = pl.multiple_of(i * 384, 128)
            over = (((1,), (1,)), ((), ()))
            both = lax.dot_general(h_hi[pl.ds(at, 384), :], cat1[...], over, preferred_element_type=F32)
            rest = lax.dot_general(h_lo[pl.ds(at, 384), :], cat1[0:WIDE, :], over, preferred_element_type=F32)
            p2[q, i] = (both[:, :WIDE] + (both[:, WIDE:] + rest)).reshape(4, OWN, WIDE)
            return carry

        lax.fori_loop(0, 2, step, 0)
        send((q, "s", 0, 1), p2.at[q, 0, at_x(2)], xr.at[q, 0, 0], x_up)
        send((q, "s", 1, 1), p2.at[q, 1, at_x(2)], xr.at[q, 1, 0], x_down)

    def reduce_1(q):
        for way, device in ((0, x_up), (1, x_down)):
            to = at_x(1) if way == 0 else at_x(3)
            arrived(q, "s", way, 1)
            xb[q, way, way] = p2[q, way, to] + xr[q, way, 0]
            xb[q, way, 1 - way] = p2[q, 1 - way, to]
            send((q, "s", way, 2), xb.at[q, way], xr.at[q, way, pl.ds(1, 2)], device)

    def reduce_2(q):
        arrived(q, "s", 0, 2)
        arrived(q, "s", 1, 2)
        for half in range(2):
            p2[q, half, x] = p2[q, half, x] + (xr[q, 0, 1 + half] + xr[q, 1, 1 + half])
        send((q, "l"), p2.at[q, 1 - y_lo, x], lr.at[q], y_near)

    def reduce_3(q):
        arrived(q, "l")
        o_ref[:, lanes(q)] = (2.0 / HALF_WIDTH) * (p2[q, y_lo, x] + lr[q]) - v_ref[:, lanes(q)]

    def split_matrix():
        offset = row * ROWS - col * COLS
        apart = lax.broadcasted_iota(jnp.int32, (16, COLS), 1) - lax.broadcasted_iota(jnp.int32, (16, COLS), 0)

        for i in range(PIECES):
            loads[i].wait()

            def step(j, carry):
                at = pl.multiple_of(i * OWN + j * 16, 16)
                inside = pl.multiple_of(j * 16, 16)
                value = h_in[i, pl.ds(inside, 16), :]
                high, low = split(value - jnp.where(apart == offset + at, F32(CENTER), F32(0.0)))
                h_hi[pl.ds(at, 16), :] = high
                h_lo[pl.ds(at, 16), :] = low
                return carry

            lax.fori_loop(0, OWN // 16, step, 0)

    stages = [
        gather_0, gather_1, gather_2, product_1, scatter_0,
        functools.partial(scatter, 2), functools.partial(scatter, 3), functools.partial(scatter, 4), scatter_y,
        spread_0, functools.partial(spread, 2), functools.partial(spread, 3), functools.partial(spread, 4), spread_last,
        product_2, reduce_1, reduce_2, reduce_3,
    ]
    plan = sorted((READY[s] + APART * q, q, s) for q in range(CHUNKS) for s in range(len(stages)))
    for q in range(CHUNKS):
        gather_0(q)
    split_pending = True
    for _, q, s in plan:
        if s == 0:
            continue
        if s == 3 and split_pending:
            split_matrix()
            split_pending = False
        stages[s](q)
    for copy in started.values():
        copy.wait_send()


def on_device(hamiltonian, vectors):
    n = CHUNKS
    copies = n * 38
    return pl.pallas_call(
        kernel,
        out_shape=jax.ShapeDtypeStruct((OWN, n * WIDE), F32),
        in_specs=[pl.BlockSpec(memory_space=pl.ANY), pl.BlockSpec(memory_space=pltpu.VMEM)],
        out_specs=pl.BlockSpec(memory_space=pltpu.VMEM),
        scratch_shapes=[
            pltpu.VMEM((PIECES, OWN, COLS), F32),
            pltpu.VMEM((ROWS, COLS), BF16),
            pltpu.VMEM((ROWS, COLS), BF16),
            pltpu.VMEM((n, 8, OWN, WIDE), F32),
            pltpu.VMEM((2 * WIDE, ROWS), BF16),
            pltpu.VMEM((n, 2, 8, 16, HALF), F32),
            pltpu.VMEM((n, 8, 16, HALF), F32),
            pltpu.VMEM((n, 2, 4, 16, HALF), F32),
            pltpu.VMEM((n, 16, HALF), F32),
            pltpu.VMEM((n, 16, HALF), F32),
            pltpu.VMEM((n, 2, 8, 16, HALF), F32),
            pltpu.VMEM((2 * WIDE, COLS), BF16),
            pltpu.VMEM((n, 2, 4, OWN, WIDE), F32),
            pltpu.VMEM((n, 2, 3, OWN, WIDE), F32),
            pltpu.VMEM((n, 2, 2, OWN, WIDE), F32),
            pltpu.VMEM((n, OWN, WIDE), F32),
            pltpu.SemaphoreType.DMA((PIECES,)),
            pltpu.SemaphoreType.DMA((copies,)),
            pltpu.SemaphoreType.DMA((copies,)),
        ],
        compiler_params=pltpu.CompilerParams(
            collective_id=0, has_side_effects=True, vmem_limit_bytes=64_000_000
        ),
    )(hamiltonian, vectors)


def solution(mesh):
    return jax.shard_map(
        on_device,
        mesh=mesh,
        in_specs=(P("row", "col"), P(("row", "col"), None)),
        out_specs=P(("row", "col"), None),
        check_vma=False,
    )
```

time: 374 us -> 136 us (0.36); the launches traced: 370 us -> 136 us
  waiting for transfers between devices: 313 us -> 0 us
  Pallas kernels: 0 us -> 134 us
  matrix products: 40 us -> 0 us
  between operations: 13.2 us -> 0.01 us
    reduce_scatter x2 -> x0, waiting for transfers between devices: 173 us -> none  [the longest x1 139 us: on_device(): lax.psum_scatter(transposed_product(shifted, row_block), 'row', scatter_d...]
    all_gather x2 -> x0, waiting for transfers between devices: 139 us -> none  [the longest x1 97 us: on_device(): lax.all_gather(recent, 'row', axis=0, tiled=True)]
    pallas_call x0 -> x1, Pallas kernels: none -> 134 us  [on_device(): pl.pallas_call(kernel, out_shape=jax.ShapeDtypeStruct((OWN, n * WIDE), F3...]
    dot_general x2 -> x0, matrix products: 40 us -> none  [the longest x1 20.2 us: plain_product(): jnp.dot(left, right, precision=lax.Precision.HIGHEST, preferred_element_t...]
  transfers between devices with their start and end apart: 4 -> 0, of which waited for: 4 -> 0; matrix products, arithmetic and copies ran while one was open for 0% -> 0% of each run, Pallas kernels for 0% -> 0%
where the time goes in v1:
time: 136 us
  Pallas kernels  134 us (99%)
  local copies, waits for them, and re-layouts  1.62 us (1%)
    pallas_call x1, Pallas kernels, on_device(): pl.pallas_call(kernel, out_shape=jax.ShapeDtypeStruct((OWN, n * WIDE), F3...  134 us

profile of v1, /device:TPU:1, one launch (start us, length us, event | category | flops | bytes accessed | tf_op | source)
XLA Modules:
  0.0 135.9 jit_solution(13799195966568249254)
XLA Ops:
  0.0 134.3 %shard_map.28 = f32[96,512]{1,0:T(8,128)} custom-call(f32[768,3072]{1,0:T(8,128)} %h_ref.1, f32[96,512]{1,0:T(8,128)} %v_ref.1), custom_call_target="tpu_custom_call" | custom-call | tf_op jit(solution)/shard_map/pallas_call | solution.py:261
  134.3 1.6 %copy.4 = f32[96,512]{1,0:T(8,128)} copy(f32[96,512]{1,0:T(8,128)} %shard_map.28) | data formatting | bytes 393216

commit v2 on v0

v2 whole, which is shorter than its diff:
```python
import functools

import jax
import jax.numpy as jnp
from jax import lax
from jax.experimental import pallas as pl
from jax.experimental.pallas import tpu as pltpu
from jax.sharding import PartitionSpec as P

MESH = pl.DeviceIdType.MESH
F32 = jnp.float32
BF16 = jnp.bfloat16

CENTER = 0.6
HALF_WIDTH = 1.8

CHUNKS = 4
WIDE = 128
ROWS, COLS = 768, 3072
HALF = COLS // 2
STREAMS = 2
LANES = HALF // STREAMS
OWN = 96
PIECES = 8

MODES = ("zy", "yz", "zy", "yz")

HOP = {
    "z_up": 3.0, "z_down": 3.0, "x_up": 3.0, "x_down": 3.0, "x_far": 3.6, "y_near": 2.4, "y_far": 3.4, "sibling": 0.9,
    "xy_up": 3.7, "xy_down": 3.7, "xy_far": 4.3,
}
LINES = {
    "x_far": ("x_up", "x_down"), "y_near": ("y",), "y_far": ("y",),
    "xy_up": ("x_up", "y"), "xy_down": ("x_down", "y"), "xy_far": ("x_up", "x_down", "y"),
}
RATE = {"sibling": 500e3}
LINK_RATE = 46.5e3
BEGIN = 7.0
SPLIT, TURN, PRODUCT_1, PRODUCT_2, CONVERT = 0.8, 0.4, 2.1, 2.3, 0.4


def split(value):
    high = value.astype(BF16)
    return high, (value - high.astype(F32)).astype(BF16)


def ordered(tasks):
    now, free, landed, done, names = BEGIN, {}, {}, {}, []
    left = dict(tasks)
    while left:
        best, soonest = None, None
        for name, (rank, needs, _, _, _) in left.items():
            times = [landed.get(need[1:]) if need[0] == "m" else done.get(need) for need in needs]
            if None in times:
                continue
            at = max(times, default=0.0)
            if at > now:
                soonest = at if soonest is None else min(soonest, at)
            elif best is None or rank < best[0]:
                best = (rank, name)
        if best is None:
            now = soonest
            continue
        name = best[1]
        _, _, cost, messages, _ = left.pop(name)
        now += cost
        done[name] = now
        names.append(name)
        for key, link, size, _ in messages:
            lines = LINES.get(link, (link,))
            end = max([now] + [free.get(line, 0.0) for line in lines]) + size / RATE.get(link, LINK_RATE)
            free.update((line, end) for line in lines)
            landed[key] = end + HOP[link]
    return names


def kernel(h_ref, v_ref, o_ref, h_in, h_hi, h_lo, y0, cat0, p1, cr, fr, zr, yb, yr, y1, cat1, p2, xr, lr,
           h_sem, send_sem, recv_sem):
    row, col = lax.axis_index("row"), lax.axis_index("col")
    core, z, y_hi = lax.rem(row, 2), lax.rem(row // 2, 8), row // 16
    x, y_lo = lax.rem(col, 4), col // 4

    def at_z(k):
        return lax.rem(z + k, 8)

    def at_x(k):
        return lax.rem(x + k, 4)

    device = {
        "z_up": (y_hi * 16 + at_z(1) * 2 + core, col),
        "z_down": (y_hi * 16 + at_z(7) * 2 + core, col),
        "sibling": (row + 1 - 2 * core, col),
        "y_far": (lax.rem(row + 16, 32), col),
        "x_up": (row, y_lo * 4 + at_x(1)),
        "x_down": (row, y_lo * 4 + at_x(3)),
        "x_far": (row, y_lo * 4 + at_x(2)),
        "y_near": (row, lax.rem(col + 4, 8)),
        "xy_up": (row, (1 - y_lo) * 4 + at_x(1)),
        "xy_down": (row, (1 - y_lo) * 4 + at_x(3)),
        "xy_far": (row, (1 - y_lo) * 4 + at_x(2)),
    }
    around_z = ("z_up", "z_down")
    along_x = ("x_up", "x_down", "x_far")
    across = ("y_near", "xy_up", "xy_down", "xy_far")
    x_of = {"x_up": 1, "x_down": 3, "x_far": 2, "y_near": 0, "xy_up": 1, "xy_down": 3, "xy_far": 2}

    loads = [
        pltpu.make_async_copy(h_ref.at[pl.ds(OWN * i, OWN), :], h_in.at[i], h_sem.at[i]) for i in range(PIECES)
    ]
    for load in loads:
        load.start()

    barrier = pltpu.get_barrier_semaphore()
    for partner in device.values():
        pl.semaphore_signal(barrier, inc=1, device_id=partner, device_id_type=MESH)
    pl.semaphore_wait(barrier, len(device))

    tasks = {}

    def add(name, needs, cost, body=None, messages=(), rank=0):
        tasks[name] = ((rank, name[1]), needs, cost, messages, body)

    def lanes(q):
        return pl.ds(WIDE * q, WIDE)

    offset = row * ROWS - col * COLS
    apart = lax.broadcasted_iota(jnp.int32, (16, COLS), 1) - lax.broadcasted_iota(jnp.int32, (16, COLS), 0)

    def split_piece(i):
        loads[i].wait()

        def step(j, carry):
            at = pl.multiple_of(i * OWN + j * 16, 16)
            value = h_in[i, pl.ds(pl.multiple_of(j * 16, 16), 16), :]
            high, low = split(value - jnp.where(apart == offset + at, F32(CENTER), F32(0.0)))
            h_hi[pl.ds(at, 16), :] = high
            h_lo[pl.ds(at, 16), :] = low
            return carry

        lax.fori_loop(0, OWN // 16, step, 0)

    for i in range(PIECES):
        add(("split", i), [], SPLIT, functools.partial(split_piece, i), rank=9)
    all_split = [("split", i) for i in range(PIECES)]

    def chunk(q):
        def msg(*key):
            return ("m", q, *key)

        size = OWN * WIDE * 4

        def own():
            return v_ref.at[:, lanes(q)], y0.at[q, col]

        def other():
            ref = y0.at[q, lax.rem(col + 4, 8)]
            return ref, ref

        def keep_own():
            y0[q, col] = v_ref[:, lanes(q)]

        before = [("A1", q - 1) if q > 1 else ("A0", 0)] if q else []
        if q == 0:
            add(("A0", q), before, 0.1, keep_own, [((q, "a", link), link, size, own) for link in along_x + across])
            gathered = [msg("a", link) for link in along_x + across]
        else:
            add(("A0", q), before, 0.1, keep_own, [((q, "a", link), link, size, own) for link in ("y_near",) + along_x])
            add(("A1", q), [msg("a", "y_near")], 0.02, None,
                [((q, "b", link), link, size, other) for link in along_x])
            gathered = [msg(kind, link) for kind in "ab" for link in along_x]

        def turn():
            high, low = split(y0[q].reshape(ROWS, WIDE).T)
            cat0[0:WIDE, :] = high
            cat0[WIDE:, :] = low

        add(("T", q), gathered + all_split + ([("M1", q - 1, 1, STREAMS - 1)] if q else []),
            TURN, turn, rank=2)

        def product_1(h, u):
            half = core if h else 1 - core

            at = pl.ds(pl.multiple_of(half * HALF + u * LANES, 128), LANES)
            both = jnp.dot(cat0[...], h_hi[:, at], preferred_element_type=F32)
            rest = jnp.dot(cat0[0:WIDE, :], h_lo[:, at], preferred_element_type=F32)
            p1[q, half, u] = (both[:WIDE] + (both[WIDE:] + rest)).reshape(8, 2, 8, LANES)

        last = ("T", q)
        for h in range(2):
            for u in range(STREAMS):
                over = []
                if h == 0:
                    refs = functools.partial(lambda u: (p1.at[q, 1 - core, u], cr.at[q, u]), u)
                    over = [((q, "c", u), "sibling", WIDE * LANES * 4, refs)]
                add(("M1", q, h, u), [last], PRODUCT_1 / 2 / STREAMS, functools.partial(product_1, h, u), over, rank=2)
                last = ("M1", q, h, u)

        blocks = {}
        for u in range(STREAMS):
            blocks[0, u], blocks[1, u] = stream(q, u, msg)

        begun = []

        def product_2(h, u):
            half = 1 - core if h else core
            high, low = split(y1[q, half, u].reshape(WIDE, LANES))
            cat1[0:WIDE, :] = high
            cat1[WIDE:, :] = low
            columns = pl.ds(pl.multiple_of(half * HALF + u * LANES, 128), LANES)
            first = not begun
            begun.append(u)

            over = (((1,), (1,)), ((), ()))
            both = lax.dot_general(h_hi[:, columns], cat1[...], over, preferred_element_type=F32)
            rest = lax.dot_general(h_lo[:, columns], cat1[0:WIDE, :], over, preferred_element_type=F32)
            value = (both[:, :WIDE] + (both[:, WIDE:] + rest)).reshape(2, 4, OWN, WIDE)
            p2[q] = value if first else p2[q] + value

        for (h, u), needs in blocks.items():
            add(("M2", q, h, u), needs + all_split, (CONVERT + PRODUCT_2) / 2 / STREAMS,
                functools.partial(product_2, h, u), rank=1)

        products = [("M2", q, *at) for at in blocks]

        def apart_of(link, index):
            half = 1 - y_lo if link in across else y_lo
            return p2.at[q, half, at_x(x_of[link])], lr.at[q, index]

        def both_of(link, index):
            return p2.at[q, :, at_x(x_of[link])], xr.at[q, index]

        if q == CHUNKS - 1:
            links = along_x + across
            add(("S1", q), products, 0.05, None, [
                ((q, "s", link), link, size, functools.partial(apart_of, link, i)) for i, link in enumerate(links)
            ])

            def finish():
                value = p2[q, y_lo, x]
                for i in range(len(links)):
                    value = value + lr[q, i]
                o_ref[:, lanes(q)] = (2.0 / HALF_WIDTH) * value - v_ref[:, lanes(q)]

            add(("S4", q), [msg("s", link) for link in links], 0.1, finish)
            return

        add(("S1", q), products, 0.05, None, [
            ((q, "s", link), link, 2 * size, functools.partial(both_of, link, i)) for i, link in enumerate(along_x)
        ])

        def reduce_x():
            for half in range(2):
                p2[q, half, x] = (p2[q, half, x] + xr[q, 0, half]) + (xr[q, 1, half] + xr[q, 2, half])

        def reduce_y():
            o_ref[:, lanes(q)] = (2.0 / HALF_WIDTH) * (p2[q, y_lo, x] + lr[q, 0]) - v_ref[:, lanes(q)]

        add(("S3", q), [msg("s", link) for link in along_x], 0.1, reduce_x,
            [((q, "l"), "y_near", size, lambda: (p2.at[q, 1 - y_lo, x], lr.at[q, 0]))])
        add(("S4", q), [msg("l")], 0.06, reduce_y)

    count = {"z": 0, "y": 0}

    def stream(q, u, msg):
        mode = MODES[q][u]
        far = count[mode] % 2
        count[mode] += 1
        sheet = 8 * LANES * 4
        size = 2 * sheet if mode == "z" else sheet

        def part(ref, k):
            return ref.at[q, core, u, at_z(k)] if mode == "z" else ref.at[q, core, u, at_z(k), y_hi]

        def slot(way, step):
            return zr.at[q, u, way, step - 1] if mode == "z" else zr.at[q, u, way, step - 1, 0]

        def local(k):
            if mode == "z":
                return p1[q, core, u, at_z(k)] + cr[q, u, at_z(k)]
            return p1[q, core, u, at_z(k), y_hi] + cr[q, u, at_z(k), y_hi] + fr[q, u, at_z(k)]

        needs = [msg("c", u), ("M1", q, 1, u)]
        if mode == "y":
            def give():
                p1[q, core, u, :, 1 - y_hi] = p1[q, core, u, :, 1 - y_hi] + cr[q, u, :, 1 - y_hi]

            add(("Y", q, u), needs, 0.3, give,
                [((q, "f", u), "y_far", 8 * sheet, lambda: (p1.at[q, core, u, :, 1 - y_hi], fr.at[q, u]))])
            needs = [msg("f", u)]

        def ring(way, step):
            k = 5 - step if way == 0 else 3 + step
            value = local(k)
            if step > 2 or (step == 2 and way == far):
                value = value + slot(way, step - 1)[...]
            part(p1, k)[...] = value

        def to_ring(way, step):
            k = 5 - step if way == 0 else 3 + step
            return ((q, "r", u, way, step), around_z[way], size, lambda: (part(p1, k), slot(way, step)))

        add(("R", q, u, far, 1), needs, 0.12, functools.partial(ring, far, 1), [to_ring(far, 1)])
        for way in range(2):
            for step in (2, 3, 4):
                before = needs if step == 2 and way != far else [msg("r", u, way, step - 1)]
                add(("R", q, u, way, step), before, 0.1, functools.partial(ring, way, step), [to_ring(way, step)])

        def total():
            return local(0) + (slot(0, 4)[...] + slot(1, 4)[...])

        needs = [msg("r", u, 0, 4), msg("r", u, 1, 4)]
        if mode == "z":
            def meet():
                yb[q, u] = total()

            add(("RY", q, u), needs, 0.1, meet, [((q, "y", u), "y_far", size, lambda: (yb.at[q, u], yr.at[q, u]))])
            needs = [msg("y", u)]

        def settle():
            value = yb[q, u] + yr[q, u] if mode == "z" else total()
            part(y1, 0)[...] = value * (1.0 / HALF_WIDTH)

        def whole(k):
            return y1.at[q, core, u, at_z(k)]

        def twice(make, k):
            def refs():
                ref = make(k)
                return ref, ref

            return refs

        on = functools.partial(part, y1)

        def also(k):
            if mode == "z":
                return [((q, "d", u, k), "sibling", size, twice(whole, k))]
            return [((q, "v", u, k), "y_far", size, twice(on, k))]

        def onward(way, step, k):
            return ((q, "g", u, way, step), around_z[way], size, twice(on, k))

        add(("G", q, u), needs, 0.1, settle, [onward(0, 1, 0), onward(1, 1, 0)] + also(0))
        holder = {0: ("G", q, u)}
        for way in range(2):
            for step in (1, 2, 3, 4):
                if step == 4 and way != far:
                    continue
                k = (8 - step) % 8 if way == 0 else step
                further = [onward(way, step + 1, k)] if step < 3 or (step == 3 and way == far) else []
                add(("F", q, u, way, step), [msg("g", u, way, step)], 0.03, None, further + also(k))
                holder[k] = ("F", q, u, way, step)
        if mode == "y":
            for k in range(8):
                add(("V", q, u, k), [msg("v", u, k), holder[k]], 0.02, None,
                    [((q, "d", u, k), "sibling", 2 * size, twice(whole, k))])
                holder[k] = ("V", q, u, k)
        return list(holder.values()), [msg("d", u, k) for k in range(8)]

    for q in range(CHUNKS):
        chunk(q)

    copies, waited = {}, set()
    for name in ordered(tasks):
        _, needs, _, messages, body = tasks[name]
        for need in needs:
            if need[0] == "m" and need not in waited:
                waited.add(need)
                copies[need[1:]].wait_recv()
        if body is not None:
            body()
        for key, link, _, refs in messages:
            src, dst = refs()
            copy = pltpu.make_async_remote_copy(
                src_ref=src, dst_ref=dst, send_sem=send_sem.at[len(copies)], recv_sem=recv_sem.at[len(copies)],
                device_id=device[link], device_id_type=MESH,
            )
            copy.start()
            copies[key] = copy
    for copy in copies.values():
        copy.wait_send()


def on_device(hamiltonian, vectors):
    n = CHUNKS
    modes = "".join(MODES)
    copies = n * (7 + STREAMS + 4) + 3 + 23 * modes.count("z") + 31 * modes.count("y")
    return pl.pallas_call(
        kernel,
        out_shape=jax.ShapeDtypeStruct((OWN, n * WIDE), F32),
        in_specs=[pl.BlockSpec(memory_space=pl.ANY), pl.BlockSpec(memory_space=pltpu.VMEM)],
        out_specs=pl.BlockSpec(memory_space=pltpu.VMEM),
        scratch_shapes=[
            pltpu.VMEM((PIECES, OWN, COLS), F32),
            pltpu.VMEM((ROWS, COLS), BF16),
            pltpu.VMEM((ROWS, COLS), BF16),
            pltpu.VMEM((n, 8, OWN, WIDE), F32),
            pltpu.VMEM((2 * WIDE, ROWS), BF16),
            pltpu.VMEM((n, 2, STREAMS, 8, 2, 8, LANES), F32),
            pltpu.VMEM((n, STREAMS, 8, 2, 8, LANES), F32),
            pltpu.VMEM((n, STREAMS, 8, 8, LANES), F32),
            pltpu.VMEM((n, STREAMS, 2, 4, 2, 8, LANES), F32),
            pltpu.VMEM((n, STREAMS, 2, 8, LANES), F32),
            pltpu.VMEM((n, STREAMS, 2, 8, LANES), F32),
            pltpu.VMEM((n, 2, STREAMS, 8, 2, 8, LANES), F32),
            pltpu.VMEM((2 * WIDE, LANES), BF16),
            pltpu.VMEM((n, 2, 4, OWN, WIDE), F32),
            pltpu.VMEM((n, 3, 2, OWN, WIDE), F32),
            pltpu.VMEM((n, 7, OWN, WIDE), F32),
            pltpu.SemaphoreType.DMA((PIECES,)),
            pltpu.SemaphoreType.DMA((copies,)),
            pltpu.SemaphoreType.DMA((copies,)),
        ],
        compiler_params=pltpu.CompilerParams(
            collective_id=0, has_side_effects=True, vmem_limit_bytes=64_000_000
        ),
    )(hamiltonian, vectors)


def solution(mesh):
    return jax.shard_map(
        on_device,
        mesh=mesh,
        in_specs=(P("row", "col"), P(("row", "col"), None)),
        out_specs=P(("row", "col"), None),
        check_vma=False,
    )
```

time: 374 us -> 101 us (0.27)
  waiting for transfers between devices: 313 us -> 0 us
  Pallas kernels: 0 us -> 99.1 us
  matrix products: 40 us -> 0 us
  between operations: 13.2 us -> 0.01 us
    reduce_scatter x2 -> x0, waiting for transfers between devices: 173 us -> none  [the longest x1 139 us: on_device(): lax.psum_scatter(transposed_product(shifted, row_block), 'row', scatter_d...]
    all_gather x2 -> x0, waiting for transfers between devices: 139 us -> none  [the longest x1 97 us: on_device(): lax.all_gather(recent, 'row', axis=0, tiled=True)]
    pallas_call x0 -> x1, Pallas kernels: none -> 99.1 us  [on_device(): pl.pallas_call(kernel, out_shape=jax.ShapeDtypeStruct((OWN, n * WIDE), F3...]
    dot_general x2 -> x0, matrix products: 40 us -> none  [the longest x1 20.2 us: plain_product(): jnp.dot(left, right, precision=lax.Precision.HIGHEST, preferred_element_t...]
  transfers between devices with their start and end apart: 4 -> 0, of which waited for: 4 -> 0; matrix products, arithmetic and copies ran while one was open for 0% -> 0% of each run, Pallas kernels for 0% -> 0%
where the time goes in v2:
time: 101 us
  Pallas kernels  99.1 us (98%)
  local copies, waits for them, and re-layouts  1.62 us (2%)
    pallas_call x1, Pallas kernels, on_device(): pl.pallas_call(kernel, out_shape=jax.ShapeDtypeStruct((OWN, n * WIDE), F3...  99.1 us

profile of v2, /device:TPU:1, one launch (start us, length us, event | category | flops | bytes accessed | tf_op | source)
XLA Modules:
  0.0 100.7 jit_solution(16376996876249491039)
XLA Ops:
  0.0 99.1 %shard_map.28 = f32[96,512]{1,0:T(8,128)} custom-call(f32[768,3072]{1,0:T(8,128)} %h_ref.1, f32[96,512]{1,0:T(8,128)} %v_ref.1), custom_call_target="tpu_custom_call" | custom-call | tf_op jit(solution)/shard_map/pallas_call | solution.py:388
  99.1 1.6 %copy.4 = f32[96,512]{1,0:T(8,128)} copy(f32[96,512]{1,0:T(8,128)} %shard_map.28) | data formatting | bytes 393216

commit v3 on v2

--- a/solution.py
+++ b/solution.py
@@ -23,7 +23,22 @@
 OWN = 96
 PIECES = 8
 
-MODES = ("zy", "yz", "zy", "yz")
+MODES = ("yz", "yz", "yz", "yz")
+GATHER = "dyyy"
+SUMS = "xxxd"
+
+ORDER = (
+    8, 4, 7, 2, 1, 5, 6, 62, 0, 3, 63, 116, 10, 11, 12, 13, 117, 170, 15, 14, 39, 43, 64, 65,
+    66, 67, 68, 171, 69, 44, 40, 94, 93, 118, 119, 120, 121, 122, 16, 123, 20, 147, 151, 41, 45, 172, 97, 95,
+    173, 174, 17, 70, 71, 175, 21, 148, 177, 152, 176, 201, 202, 42, 18, 74, 98, 128, 124, 72, 9, 153, 149, 22,
+    96, 46, 75, 205, 19, 125, 178, 179, 129, 99, 203, 73, 76, 23, 126, 150, 47, 182, 180, 206, 100, 130, 77, 127,
+    28, 24, 52, 154, 204, 183, 207, 48, 181, 81, 29, 131, 25, 78, 101, 184, 155, 208, 53, 49, 30, 82, 26, 132,
+    32, 136, 185, 79, 105, 38, 156, 209, 33, 27, 83, 133, 50, 160, 54, 31, 189, 87, 102, 37, 86, 140, 106, 91,
+    193, 137, 213, 146, 157, 80, 36, 35, 84, 134, 34, 55, 186, 51, 194, 190, 56, 103, 210, 107, 57, 58, 59, 85,
+    88, 158, 161, 90, 92, 135, 214, 89, 109, 144, 187, 191, 110, 200, 104, 138, 108, 111, 112, 141, 211, 113, 188, 139,
+    143, 215, 162, 192, 145, 195, 159, 165, 199, 196, 142, 163, 166, 164, 167, 216, 212, 197, 60, 219, 198, 220, 217, 218,
+    114, 221, 61, 168, 115, 169, 222,
+)
 
 HOP = {
     "z_up": 3.0, "z_down": 3.0, "x_up": 3.0, "x_down": 3.0, "x_far": 3.6, "y_near": 2.4, "y_far": 3.4, "sibling": 0.9,
@@ -74,8 +89,8 @@
     return names
 
 
-def kernel(h_ref, v_ref, o_ref, h_in, h_hi, h_lo, y0, cat0, p1, cr, fr, zr, yb, yr, y1, cat1, p2, xr, lr,
-           h_sem, send_sem, recv_sem):
+def kernel(h_ref, v_ref, o_ref, v_in, out, h_in, h_hi, h_lo, y0, cat0, p1, cr, fr, zr, yb, yr, y1, cat1, p2, xr, lr, nr,
+           v_sem, o_sem, h_sem, send_sem, recv_sem):
     row, col = lax.axis_index("row"), lax.axis_index("col")
     core, z, y_hi = lax.rem(row, 2), lax.rem(row // 2, 8), row // 16
     x, y_lo = lax.rem(col, 4), col // 4
@@ -104,6 +119,8 @@
     across = ("y_near", "xy_up", "xy_down", "xy_far")
     x_of = {"x_up": 1, "x_down": 3, "x_far": 2, "y_near": 0, "xy_up": 1, "xy_down": 3, "xy_far": 2}
 
+    v_load = pltpu.make_async_copy(v_ref, v_in, v_sem)
+    v_load.start()
     loads = [
         pltpu.make_async_copy(h_ref.at[pl.ds(OWN * i, OWN), :], h_in.at[i], h_sem.at[i]) for i in range(PIECES)
     ]
@@ -152,24 +169,32 @@
         def own():
             return v_ref.at[:, lanes(q)], y0.at[q, col]
 
-        def other():
-            ref = y0.at[q, lax.rem(col + 4, 8)]
+        def slice_of(half, k):
+            ref = y0.at[q, (y_lo + half - 2 * half * y_lo) * 4 + at_x(k)]
             return ref, ref
 
-        def keep_own():
-            y0[q, col] = v_ref[:, lanes(q)]
-
-        before = [("A1", q - 1) if q > 1 else ("A0", 0)] if q else []
-        if q == 0:
-            add(("A0", q), before, 0.1, keep_own, [((q, "a", link), link, size, own) for link in along_x + across])
+        before = [("A0", 0)] if q == 1 else [("A1", q - 1)] if q else []
+        if GATHER[q] == "d":
+            add(("A0", q), before, 0.1, None, [((q, "a", link), link, size, own) for link in along_x + across])
+            add(("A1", q), [("A0", q)], 0.0)
             gathered = [msg("a", link) for link in along_x + across]
         else:
-            add(("A0", q), before, 0.1, keep_own, [((q, "a", link), link, size, own) for link in ("y_near",) + along_x])
-            add(("A1", q), [msg("a", "y_near")], 0.02, None,
-                [((q, "b", link), link, size, other) for link in along_x])
-            gathered = [msg(kind, link) for kind in "ab" for link in along_x]
+            add(("A0", q), before, 0.1, None, [((q, "a", link), link, size, own) for link in ("y_near",) + along_x])
+            if GATHER[q] == "y":
+                add(("A1", q), [msg("a", "y_near")], 0.02, None,
+                    [((q, "b", link), link, size, functools.partial(slice_of, 1, 0)) for link in along_x])
+            else:
+                for n, link in enumerate(along_x):
+                    k = (4 - x_of[link]) % 4
+                    add(("A%d" % (n + 1), q), [msg("a", link)], 0.02, None,
+                        [((q, "b", link), "y_near", size, functools.partial(slice_of, 0, k))])
+            gathered = [msg("a", link) for link in ("y_near",) + along_x] + [msg("b", link) for link in along_x]
 
         def turn():
+            if not turned:
+                v_load.wait()
+            turned.append(q)
+            y0[q, col] = v_in[:, lanes(q)]
             high, low = split(y0[q].reshape(ROWS, WIDE).T)
             cat0[0:WIDE, :] = high
             cat0[WIDE:, :] = low
@@ -229,7 +254,7 @@
         def both_of(link, index):
             return p2.at[q, :, at_x(x_of[link])], xr.at[q, index]
 
-        if q == CHUNKS - 1:
+        if SUMS[q] == "d":
             links = along_x + across
             add(("S1", q), products, 0.05, None, [
                 ((q, "s", link), link, size, functools.partial(apart_of, link, i)) for i, link in enumerate(links)
@@ -239,9 +264,27 @@
                 value = p2[q, y_lo, x]
                 for i in range(len(links)):
                     value = value + lr[q, i]
-                o_ref[:, lanes(q)] = (2.0 / HALF_WIDTH) * value - v_ref[:, lanes(q)]
+                put(q, value)
 
             add(("S4", q), [msg("s", link) for link in links], 0.1, finish)
+            return
+
+        if SUMS[q] == "y":
+            def reduce_near():
+                p2[q, y_lo] = p2[q, y_lo] + nr[q]
+
+            def near_of(link, index):
+                return p2.at[q, y_lo, at_x(x_of[link])], lr.at[q, index]
+
+            def finish_near():
+                value = (p2[q, y_lo, x] + lr[q, 0]) + (lr[q, 1] + lr[q, 2])
+                put(q, value)
+
+            add(("S1", q), products, 0.05, None,
+                [((q, "l"), "y_near", 4 * size, lambda: (p2.at[q, 1 - y_lo], nr.at[q]))])
+            add(("S3", q), [msg("l")], 0.15, reduce_near,
+                [((q, "s", link), link, size, functools.partial(near_of, link, i)) for i, link in enumerate(along_x)])
+            add(("S4", q), [msg("s", link) for link in along_x], 0.1, finish_near)
             return
 
         add(("S1", q), products, 0.05, None, [
@@ -253,13 +296,19 @@
                 p2[q, half, x] = (p2[q, half, x] + xr[q, 0, half]) + (xr[q, 1, half] + xr[q, 2, half])
 
         def reduce_y():
-            o_ref[:, lanes(q)] = (2.0 / HALF_WIDTH) * (p2[q, y_lo, x] + lr[q, 0]) - v_ref[:, lanes(q)]
+            put(q, p2[q, y_lo, x] + lr[q, 0])
 
         add(("S3", q), [msg("s", link) for link in along_x], 0.1, reduce_x,
             [((q, "l"), "y_near", size, lambda: (p2.at[q, 1 - y_lo, x], lr.at[q, 0]))])
         add(("S4", q), [msg("l")], 0.06, reduce_y)
 
-    count = {"z": 0, "y": 0}
+    count, turned, stores = {"z": 0, "y": 0}, [], []
+
+    def put(q, total):
+        out[q] = (2.0 / HALF_WIDTH) * total - v_in[:, lanes(q)]
+        store = pltpu.make_async_copy(out.at[q], o_ref.at[:, lanes(q)], o_sem.at[q])
+        store.start()
+        stores.append(store)
 
     def stream(q, u, msg):
         mode = MODES[q][u]
@@ -361,7 +410,8 @@
         chunk(q)
 
     copies, waited = {}, set()
-    for name in ordered(tasks):
+    every = list(tasks)
+    for name in [every[i] for i in ORDER]:
         _, needs, _, messages, body = tasks[name]
         for need in needs:
             if need[0] == "m" and need not in waited:
@@ -379,18 +429,22 @@
             copies[key] = copy
     for copy in copies.values():
         copy.wait_send()
+    for store in stores:
+        store.wait()
 
 
 def on_device(hamiltonian, vectors):
     n = CHUNKS
     modes = "".join(MODES)
-    copies = n * (7 + STREAMS + 4) + 3 + 23 * modes.count("z") + 31 * modes.count("y")
+    copies = n * (7 + STREAMS + 4) + 3 * SUMS.count("d") + 23 * modes.count("z") + 31 * modes.count("y")
     return pl.pallas_call(
         kernel,
         out_shape=jax.ShapeDtypeStruct((OWN, n * WIDE), F32),
-        in_specs=[pl.BlockSpec(memory_space=pl.ANY), pl.BlockSpec(memory_space=pltpu.VMEM)],
-        out_specs=pl.BlockSpec(memory_space=pltpu.VMEM),
+        in_specs=[pl.BlockSpec(memory_space=pl.ANY)] * 2,
+        out_specs=pl.BlockSpec(memory_space=pl.ANY),
         scratch_shapes=[
+            pltpu.VMEM((OWN, n * WIDE), F32),
+            pltpu.VMEM((n, OWN, WIDE), F32),
             pltpu.VMEM((PIECES, OWN, COLS), F32),
             pltpu.VMEM((ROWS, COLS), BF16),
             pltpu.VMEM((ROWS, COLS), BF16),
@@ -407,12 +461,15 @@
             pltpu.VMEM((n, 2, 4, OWN, WIDE), F32),
             pltpu.VMEM((n, 3, 2, OWN, WIDE), F32),
             pltpu.VMEM((n, 7, OWN, WIDE), F32),
+            pltpu.VMEM((n, 4, OWN, WIDE), F32),
+            pltpu.SemaphoreType.DMA,
+            pltpu.SemaphoreType.DMA((n,)),
             pltpu.SemaphoreType.DMA((PIECES,)),
             pltpu.SemaphoreType.DMA((copies,)),
             pltpu.SemaphoreType.DMA((copies,)),
         ],
         compiler_params=pltpu.CompilerParams(
-            collective_id=0, has_side_effects=True, vmem_limit_bytes=64_000_000
+            collective_id=0, has_side_effects=True, vmem_limit_bytes=66_000_000
         ),
     )(hamiltonian, vectors)
 

time: 101 us -> 96.7 us (0.957)
  Pallas kernels: 99.1 us -> 95 us
    pallas_call x1, Pallas kernels: 99.1 us -> 95 us  [on_device(): pl.pallas_call(kernel, out_shape=jax.ShapeDtypeStruct((OWN, n * WIDE), F3...]
where the time goes in v3:
time: 96.7 us; the launch traced here: 96.6 us
  Pallas kernels  95 us (98%)
  local copies, waits for them, and re-layouts  1.62 us (2%)
    pallas_call x1, Pallas kernels, on_device(): pl.pallas_call(kernel, out_shape=jax.ShapeDtypeStruct((OWN, n * WIDE), F3...  95 us

profile of v3, /device:TPU:1, one launch (start us, length us, event | category | flops | bytes accessed | tf_op | source)
XLA Modules:
  0.0 96.6 jit_solution(11091848060822985505)
XLA Ops:
  0.0 95.0 %shard_map.28 = f32[96,512]{1,0:T(8,128)} custom-call(f32[768,3072]{1,0:T(8,128)} %h_ref.1, f32[96,512]{1,0:T(8,128)} %v_ref.1), custom_call_target="tpu_custom_call" | custom-call | tf_op jit(solution)/shard_map/pallas_call | solution.py:440
  95.0 1.6 %copy.4 = f32[96,512]{1,0:T(8,128)} copy(f32[96,512]{1,0:T(8,128)} %shard_map.28) | data formatting | bytes 393216

commit v4 on v3

--- a/solution.py
+++ b/solution.py
@@ -23,21 +23,21 @@
 OWN = 96
 PIECES = 8
 
-MODES = ("yz", "yz", "yz", "yz")
+MODES = ("zy", "yz", "zy", "yz")
 GATHER = "dyyy"
 SUMS = "xxxd"
 
 ORDER = (
-    8, 4, 7, 2, 1, 5, 6, 62, 0, 3, 63, 116, 10, 11, 12, 13, 117, 170, 15, 14, 39, 43, 64, 65,
-    66, 67, 68, 171, 69, 44, 40, 94, 93, 118, 119, 120, 121, 122, 16, 123, 20, 147, 151, 41, 45, 172, 97, 95,
-    173, 174, 17, 70, 71, 175, 21, 148, 177, 152, 176, 201, 202, 42, 18, 74, 98, 128, 124, 72, 9, 153, 149, 22,
-    96, 46, 75, 205, 19, 125, 178, 179, 129, 99, 203, 73, 76, 23, 126, 150, 47, 182, 180, 206, 100, 130, 77, 127,
-    28, 24, 52, 154, 204, 183, 207, 48, 181, 81, 29, 131, 25, 78, 101, 184, 155, 208, 53, 49, 30, 82, 26, 132,
-    32, 136, 185, 79, 105, 38, 156, 209, 33, 27, 83, 133, 50, 160, 54, 31, 189, 87, 102, 37, 86, 140, 106, 91,
-    193, 137, 213, 146, 157, 80, 36, 35, 84, 134, 34, 55, 186, 51, 194, 190, 56, 103, 210, 107, 57, 58, 59, 85,
-    88, 158, 161, 90, 92, 135, 214, 89, 109, 144, 187, 191, 110, 200, 104, 138, 108, 111, 112, 141, 211, 113, 188, 139,
-    143, 215, 162, 192, 145, 195, 159, 165, 199, 196, 142, 163, 166, 164, 167, 216, 212, 197, 60, 219, 198, 220, 217, 218,
-    114, 221, 61, 168, 115, 169, 222,
+    8, 3, 5, 1, 9, 62, 2, 0, 6, 4, 7, 63, 116, 10, 11, 12, 13, 15, 14, 117, 170, 19, 31, 64,
+    65, 66, 16, 67, 69, 171, 68, 20, 94, 93, 32, 118, 119, 120, 36, 121, 17, 127, 123, 122, 139, 70, 33, 21,
+    95, 172, 173, 97, 174, 175, 71, 37, 18, 176, 177, 74, 140, 201, 34, 124, 144, 98, 202, 72, 38, 75, 141, 178,
+    128, 35, 179, 205, 22, 125, 96, 145, 76, 73, 182, 203, 39, 99, 142, 180, 206, 126, 129, 77, 183, 23, 146, 40,
+    204, 100, 207, 143, 181, 44, 78, 130, 184, 81, 24, 41, 28, 101, 147, 79, 208, 47, 45, 185, 25, 82, 131, 53,
+    105, 42, 148, 54, 46, 29, 102, 80, 152, 83, 189, 26, 91, 132, 209, 43, 48, 149, 106, 136, 50, 30, 84, 186,
+    103, 153, 27, 190, 86, 55, 213, 162, 87, 52, 133, 49, 51, 57, 107, 150, 56, 58, 85, 187, 137, 59, 92, 154,
+    200, 191, 88, 90, 89, 155, 210, 104, 109, 214, 161, 193, 134, 157, 110, 151, 108, 156, 111, 112, 113, 188, 160, 192,
+    138, 211, 215, 135, 158, 163, 159, 165, 164, 166, 195, 167, 212, 194, 199, 198, 196, 60, 197, 217, 216, 219, 220, 114,
+    218, 221, 168, 61, 222, 115, 169,
 )
 
 HOP = {
@@ -115,8 +115,9 @@
         "xy_far": (row, (1 - y_lo) * 4 + at_x(2)),
     }
     around_z = ("z_up", "z_down")
-    along_x = ("x_up", "x_down", "x_far")
-    across = ("y_near", "xy_up", "xy_down", "xy_far")
+    along_x = ("x_far", "x_up", "x_down")
+    across = ("xy_far", "xy_up", "xy_down", "y_near")
+    straight = ("xy_far", "x_far", "xy_up", "xy_down", "x_up", "x_down", "y_near")
     x_of = {"x_up": 1, "x_down": 3, "x_far": 2, "y_near": 0, "xy_up": 1, "xy_down": 3, "xy_far": 2}
 
     v_load = pltpu.make_async_copy(v_ref, v_in, v_sem)
@@ -175,9 +176,9 @@
 
         before = [("A0", 0)] if q == 1 else [("A1", q - 1)] if q else []
         if GATHER[q] == "d":
-            add(("A0", q), before, 0.1, None, [((q, "a", link), link, size, own) for link in along_x + across])
+            add(("A0", q), before, 0.1, None, [((q, "a", link), link, size, own) for link in straight])
             add(("A1", q), [("A0", q)], 0.0)
-            gathered = [msg("a", link) for link in along_x + across]
+            gathered = [msg("a", link) for link in straight]
         else:
             add(("A0", q), before, 0.1, None, [((q, "a", link), link, size, own) for link in ("y_near",) + along_x])
             if GATHER[q] == "y":
@@ -255,7 +256,7 @@
             return p2.at[q, :, at_x(x_of[link])], xr.at[q, index]
 
         if SUMS[q] == "d":
-            links = along_x + across
+            links = straight
             add(("S1", q), products, 0.05, None, [
                 ((q, "s", link), link, size, functools.partial(apart_of, link, i)) for i, link in enumerate(links)
             ])
@@ -333,9 +334,11 @@
             def give():
                 p1[q, core, u, :, 1 - y_hi] = p1[q, core, u, :, 1 - y_hi] + cr[q, u, :, 1 - y_hi]
 
+            def across_y(k):
+                return p1.at[q, core, u, at_z(k), 1 - y_hi], fr.at[q, u, at_z(k)]
+
             add(("Y", q, u), needs, 0.3, give,
-                [((q, "f", u), "y_far", 8 * sheet, lambda: (p1.at[q, core, u, :, 1 - y_hi], fr.at[q, u]))])
-            needs = [msg("f", u)]
+                [((q, "f", u, k), "y_far", sheet, functools.partial(across_y, k)) for k in (4, 3, 5, 2, 6, 1, 7, 0)])
 
         def ring(way, step):
             k = 5 - step if way == 0 else 3 + step
@@ -348,16 +351,21 @@
             k = 5 - step if way == 0 else 3 + step
             return ((q, "r", u, way, step), around_z[way], size, lambda: (part(p1, k), slot(way, step)))
 
-        add(("R", q, u, far, 1), needs, 0.12, functools.partial(ring, far, 1), [to_ring(far, 1)])
+        def ready(k):
+            return [msg("f", u, k)] if mode == "y" else needs
+
+        add(("R", q, u, far, 1), ready(4), 0.12, functools.partial(ring, far, 1), [to_ring(far, 1)])
         for way in range(2):
             for step in (2, 3, 4):
-                before = needs if step == 2 and way != far else [msg("r", u, way, step - 1)]
+                before = ready(5 - step if way == 0 else 3 + step)
+                if step > 2 or way == far:
+                    before = before + [msg("r", u, way, step - 1)]
                 add(("R", q, u, way, step), before, 0.1, functools.partial(ring, way, step), [to_ring(way, step)])
 
         def total():
             return local(0) + (slot(0, 4)[...] + slot(1, 4)[...])
 
-        needs = [msg("r", u, 0, 4), msg("r", u, 1, 4)]
+        needs = ready(0) + [msg("r", u, 0, 4), msg("r", u, 1, 4)]
         if mode == "z":
             def meet():
                 yb[q, u] = total()
@@ -436,7 +444,7 @@
 def on_device(hamiltonian, vectors):
     n = CHUNKS
     modes = "".join(MODES)
-    copies = n * (7 + STREAMS + 4) + 3 * SUMS.count("d") + 23 * modes.count("z") + 31 * modes.count("y")
+    copies = n * (7 + STREAMS + 4) + 3 * SUMS.count("d") + 23 * modes.count("z") + 38 * modes.count("y")
     return pl.pallas_call(
         kernel,
         out_shape=jax.ShapeDtypeStruct((OWN, n * WIDE), F32),

time: 96.7 us -> 94.7 us (0.979)
  Pallas kernels: 95 us -> 93 us
    pallas_call x1, Pallas kernels: 95 us -> 93 us  [on_device(): pl.pallas_call(kernel, out_shape=jax.ShapeDtypeStruct((OWN, n * WIDE), F3...]
where the time goes in v4:
time: 94.7 us; the launch traced here: 94.6 us
  Pallas kernels  93 us (98%)
  local copies, waits for them, and re-layouts  1.62 us (2%)
    pallas_call x1, Pallas kernels, on_device(): pl.pallas_call(kernel, out_shape=jax.ShapeDtypeStruct((OWN, n * WIDE), F3...  93 us

profile of v4, /device:TPU:1, one launch (start us, length us, event | category | flops | bytes accessed | tf_op | source)
XLA Modules:
  0.0 94.6 jit_solution(11724848743389007920)
XLA Ops:
  0.0 93.0 %shard_map.28 = f32[96,512]{1,0:T(8,128)} custom-call(f32[768,3072]{1,0:T(8,128)} %h_ref.1, f32[96,512]{1,0:T(8,128)} %v_ref.1), custom_call_target="tpu_custom_call" | custom-call | tf_op jit(solution)/shard_map/pallas_call | solution.py:448
  93.0 1.6 %copy.4 = f32[96,512]{1,0:T(8,128)} copy(f32[96,512]{1,0:T(8,128)} %shard_map.28) | data formatting | bytes 393216
